TPU v7x, 128 devices: a whole 4x4x4 slice. The times are simulated.
128 devices in a mesh: seq: 32 (over x, y, core), chan: 4 (over z).
Axes of the slice: x: 4, y: 4, z: 4, core: 2. Of those that a mesh axis runs over, the one named last changes fastest.
Arguments:
- tokens: bfloat16 [16384, 8192], P('seq'), may hold values from -6 to 6
- proj_weight: bfloat16 [8192, 3, 2048], P('seq', None, 'chan'), may hold values from -0.0625 to 0.0625
- residues: float32 [16, 2048], P(None, 'chan'), may hold values from -1.5 to 1.5
- decay_rates: float32 [16, 2048], P(None, 'chan'), may hold values from 3.0517578e-05 to 0.05
- skip_gain: float32 [2048], P('chan'), may hold values from -3 to 3
- grad_out: bfloat16 [16384, 2048], P('seq', 'chan'), may hold values from -6 to 6
Outputs:
- gated_output: bfloat16 [16384, 2048], P('seq', 'chan')
- grad_tokens: bfloat16 [16384, 8192], P('seq', 'chan')
All inputs are finite; a program needn't handle non-finite values.
Results may differ from a plain program's by a relative error of at most 0.022.
Values may be sent and summed in bfloat16 or wider, within the bound.
A program may use at most 128 MiB of HBM per device.

v0:
```python
import math
import jax
import jax.numpy as jnp
from jax import lax
from jax.sharding import PartitionSpec as P

f32 = jnp.float32
bf16 = jnp.bfloat16


def dft_tables(block_len, flip=False):
    n_len = 2 * block_len
    k = jnp.arange(block_len, dtype=jnp.int32)[:, None]
    n = jnp.arange(block_len, dtype=jnp.int32)[None, :]
    if flip:
        n = block_len - 1 - n
    phase = k * n % n_len
    angle = 2.0 * math.pi / n_len * phase.astype(f32)
    cos_rows = jnp.cos(angle)
    sin_rows = jnp.sin(angle)
    nyquist = jnp.where(n % 2 == 0, 1.0, -1.0).astype(f32)
    sin_rows = jnp.where(k == 0, nyquist, sin_rows)
    fwd = jnp.concatenate([cos_rows, sin_rows], axis=0)
    weight = jnp.where(k == 0, 1.0, 2.0).astype(f32) / n_len
    inv = jnp.concatenate([cos_rows * weight, sin_rows * weight], axis=0).T
    return (fwd, inv)


def spectral_conv(signal, fwd, inv, h_a, h_a2, h_b):
    block_len = signal.shape[0]
    spec = jnp.dot(fwd, signal.astype(bf16), preferred_element_type=f32)
    xc = spec[:block_len]
    xs = spec[block_len:]
    pr = xc * h_a - xs * h_b
    pi = xc * h_b + xs * h_a2
    prod = jnp.concatenate([pr, pi], axis=0).astype(bf16)
    return jnp.dot(inv, prod, preferred_element_type=f32)


def local(tokens, proj_weight, residues, decay_rates, skip_gain, grad_out):
    tok_rows = tokens.shape[0]
    chan_count = skip_gain.shape[0]
    seq_count = lax.axis_size(SEQ)
    me = lax.axis_index(SEQ)
    flat_w = proj_weight.reshape(proj_weight.shape[0], 3 * chan_count)
    half = 3 * chan_count // 2
    pair_w = lax.all_gather(flat_w, "core", axis=0, tiled=True)
    mine_w = lax.dynamic_slice_in_dim(pair_w, lax.axis_index("core") * half, half, axis=1)
    plane_w = lax.all_gather(mine_w, "xy", axis=0, tiled=True)
    whole_w = lax.all_gather(plane_w, "core", axis=1, tiled=True)
    projected = jnp.dot(tokens, whole_w, preferred_element_type=f32)
    proj_vals = (
        lax.optimization_barrier(projected.astype(bf16))
        .astype(f32)
        .reshape(tok_rows, 3, chan_count)
    )
    query_in = proj_vals[:, 0]
    key_in = proj_vals[:, 1]
    value_in = proj_vals[:, 2]
    mixed_in = key_in * value_in
    grad_gate = grad_out.astype(f32)
    grad_mix = grad_gate * query_in
    rates = decay_rates
    mode_gain = residues * jnp.sqrt(-jnp.expm1(-2.0 * rates))
    steps = jnp.arange(tok_rows, dtype=f32)
    fwd_w = jnp.exp(-rates[:, None, :] * (tok_rows - 1 - steps)[None, :, None])
    bwd_w = jnp.exp(-rates[:, None, :] * steps[None, :, None])
    end_fwd = jnp.sum(fwd_w * mixed_in[None], axis=1)
    end_bwd = jnp.sum(bwd_w * grad_mix[None], axis=1)
    states = jnp.stack([end_fwd, end_bwd])
    every = lax.all_gather(states, SEQ)
    others = jnp.arange(seq_count, dtype=jnp.int32)
    gap_f = me - 1 - others
    gap_b = others - me - 1
    span = rates[None] * float(tok_rows)
    w_f = jnp.where(
        (gap_f >= 0)[:, None, None],
        jnp.exp(-span * jnp.maximum(gap_f, 0).astype(f32)[:, None, None]),
        0.0,
    )
    w_b = jnp.where(
        (gap_b >= 0)[:, None, None],
        jnp.exp(-span * jnp.maximum(gap_b, 0).astype(f32)[:, None, None]),
        0.0,
    )
    into_f = jnp.sum(w_f * every[:, 0], axis=0) * mode_gain
    into_b = jnp.sum(w_b * every[:, 1], axis=0) * mode_gain
    taps = jnp.sum(mode_gain[:, None, :] * bwd_w, axis=0)
    fwd, inv = dft_tables(tok_rows)
    fwd_b = fwd.astype(bf16)
    inv_b = inv.astype(bf16)
    fwd_r, inv_r = dft_tables(tok_rows, flip=True)
    spec = jnp.dot(fwd, taps, precision=lax.Precision.HIGHEST)
    row0 = (jnp.arange(tok_rows) == 0)[:, None]
    h_a = spec[:tok_rows]
    h_a2 = jnp.where(row0, spec[tok_rows : tok_rows + 1], h_a)
    h_b = jnp.where(row0, 0.0, spec[tok_rows:])
    local_f = spectral_conv(mixed_in, fwd_b, inv_b, h_a, h_a2, h_b)
    carry_f = jnp.sum(
        into_f[:, None, :] * jnp.exp(-rates[:, None, :] * (steps + 1.0)[None, :, None]), axis=0
    )
    filtered = local_f + carry_f + skip_gain[None, :] * mixed_in
    gated_output = (query_in * filtered).astype(bf16)
    grad_query = grad_gate * filtered
    local_b = spectral_conv(grad_mix, fwd_r.astype(bf16), inv_r.astype(bf16), h_a, h_a2, h_b)
    carry_b = jnp.sum(
        into_b[:, None, :] * jnp.exp(-rates[:, None, :] * (tok_rows - steps)[None, :, None]), axis=0
    )
    grad_conv = local_b + carry_b + skip_gain[None, :] * grad_mix
    grad_proj = jnp.stack([grad_query, grad_conv * value_in, grad_conv * key_in], axis=1).astype(
        bf16
    )
    grad_proj = grad_proj.reshape(tok_rows, 3 * chan_count)
    contract = (((1,), (1,)), ((), ()))
    dx_terms = lax.dot_general(grad_proj, whole_w, contract, preferred_element_type=f32)
    grad_tokens = lax.psum_scatter(dx_terms.astype(bf16), "chan", scatter_dimension=1, tiled=True)
    return (gated_output, grad_tokens)


SEQ = ("xy", "core")


def solution(mesh):
    cores = 2
    split = jax.sharding.Mesh(
        mesh.devices.reshape(mesh.shape["seq"] // cores, cores, mesh.shape["chan"]),
        ("xy", "core", "chan"),
    )
    placed = (
        P(SEQ, None),
        P(SEQ, None, "chan"),
        P(None, "chan"),
        P(None, "chan"),
        P("chan"),
        P(SEQ, "chan"),
    )
    return jax.shard_map(
        local,
        mesh=split,
        in_specs=placed,
        out_specs=(P(SEQ, "chan"), P(SEQ, "chan")),
        check_vma=False,
    )
```

profile of v0, /device:TPU:1, one launch (start us, length us, event | category | flops | bytes accessed | tf_op | source)
XLA Modules:
  0.0 390.3 jit_solution(8192776830825825899)
XLA Ops:
  7.2 0.0 all-gather.6.cloned.1.call-start
  7.2 2.3 copy.24
  9.5 0.0 all-gather.6.cloned.1.call-update
  9.5 0.0 all-gather.8.cloned.1.call-start
  9.6 16.7 %all-gather.6.cloned.1.call-done = bf16[512,1536]{0,1:T(8,128)(2,1)} async-done(((bf16[256,1536]{0,1:T(8,128)(2,1)}), bf16[512,1536]{0,1:T(8,128)(2,1)}) %all-gather.6.cloned.1.call-update) | async-done | bytes 1572880 | tf_op jit(solution)/shard_map/all_gather | solution.py:47
  26.3 2.1 constant_dynamic-slice_fusion
  28.3 0.0 all-gather.8.cloned.1.call-update
  28.3 0.0 all-gather.10.cloned.1.call-start
  28.4 100.2 %all-gather.8.cloned.1.call-done = bf16[8192,768]{0,1:T(8,128)(2,1)} async-done(((bf16[512,768]{0,1:T(8,128)(2,1)}), bf16[8192,768]{0,1:T(8,128)(2,1)}) %all-gather.8.cloned.1.call-update) | async-done | bytes 12582928 | tf_op jit(solution)/shard_map/all_gather | solution.py:49
  128.6 0.0 all-gather.10.cloned.1.call-update
  128.6 0.0 all-gather.12.cloned.1.call-start
  128.6 1.0 copy-done.15
  129.6 1.0 copy.26
  130.6 0.0 copy-done.18
  130.6 43.3 %all-gather.10.cloned.1.call-done = bf16[8192,1536]{0,1:T(8,128)(2,1)} async-done(((bf16[8192,768]{0,1:T(8,128)(2,1)}), bf16[8192,1536]{0,1:T(8,128)(2,1)}) %all-gather.10.cloned.1.call-update) | async-done | bytes 25165840 | tf_op jit(solution)/shard_map/all_gather | solution.py:50
  174.0 19.4 %fusion = bf16[512,1536]{0,1:T(8,128)(2,1)S(1)} fusion(bf16[8192,1536]{0,1:T(8,128)(2,1)} %all-gather.10.cloned.1.call-done, bf16[512,8192]{1,0:T(8,128)(2,1)} %param.6), kind=kOutput, calls=%fused_computation.8 | convolution fusion | flops 12885688320 | bytes 35127296 | tf_op jit(solution)/shard_map/dot_general | solution.py:51
  193.3 0.0 copy-start.8
  193.4 0.4 convert.56
  193.8 0.6 copy-done.8
  194.4 1.8 convert_multiply_fusion.1
  196.1 2.6 copy.27
  198.8 2.5 copy.25
  201.3 7.2 %multiply_reduce_fusion.3 = (f32[16,512]{1,0:T(8,128)S(1)}, f32[16,512]{1,0:T(8,128)S(1)}) fusion(f32[512,512]{1,0:T(8,128)} %copy.25, f32[512]{0:T(512)S(1)} %iota_subtract_fusion.2, f32[16,512]{1,0:T(8,128)S(1)} %get-tuple-element.32, f32[512,512]{1,0:T(8,128)} %copy.27), kind=kLoop, calls=%fused_computation.3 | loop fusion | flops 25149440 | bytes 2197504 | tf_op jit(solution)/shard_map/reduce_sum | solution.py:68
  208.5 0.6 pad_maximum_fusion.3
  209.1 0.0 all-gather.12.cloned.1.call-update
  209.1 0.2 reduce-scatter.2.cloned.1.call-start
  209.5 3.8 fusion.48
  213.3 4.1 %fusion.41 = bf16[512,512]{1,0:T(8,128)(2,1)S(1)} fusion(f32[512]{0:T(512)S(1)} %fusion.57, s32[512]{0:T(512)S(1)} %iota_subtract_fusion.1, pred[512]{0:T(512)(128)(4,1)S(1)} %iota_compare_fusion), kind=kLoop, calls=%fused_computation.79 | loop fusion | flops 3932160 | bytes 528896 | tf_op jit(solution)/shard_map/convert.10
  217.4 9.7 %multiply_convert_fusion.3 = (bf16[512,512]{1,0:T(8,128)(2,1)}, bf16[512,512]{1,0:T(8,128)(2,1)}, bf16[512,512]{1,0:T(8,128)(2,1)}, f32[512,512]{1,0:T(8,128)S(1...) fusion(f32[512]{0:T(512)S(1)} %get-tuple-element.41, s32[512]{0:T(512)S(1)} %iota_subtract_fusion.1, ...), kind=kLoop, calls=%fused_computation.65 | loop fusion | flops 10223616 | bytes 3678720 | tf_op jit(solution)/shard_map/convert.11
  227.2 2.1 fusion.12
  229.2 0.0 copy-done.4
  229.2 2.1 fusion.27
  231.4 22.9 %all-gather.12.cloned.1.call-done = f32[64,16,512]{2,1,0:T(8,128)} async-done(((f32[2,16,512]{2,1,0:T(8,128)}), f32[64,16,512]{2,1,0:T(8,128)}) %all-gather.12.cloned.1.call-update) | async-done | bytes 2097168 | tf_op jit(solution)/shard_map/all_gather | solution.py:71
  254.3 2.1 fusion.15
  256.4 0.0 copy-done.19
  256.4 10.7 %multiply_reduce_fusion = (f32[512,512]{1,0:T(8,128)}, f32[512,512]{1,0:T(8,128)}, f32[512,512]{1,0:T(8,128)}) fusion(f32[512]{0:T(512)S(1)} %get-tuple-element.39, f32[16,512]{1,0:T(8,128)S(1)} %mul.373, f32[16,512]{1,0:T(8,128)S(1)} %get-tuple-element.32, f32[512]{0:T(512)S(1)} %get-tuple-element.40, f32[16,512]{1,0:T(8,128)S(1)} %get-tuple-element.17, ...), kind=kLoop, calls=%fused_computation | loop fusion | flops 36962304 | bytes 3280896 | tf_op jit(solution)/shard_map/reduce_sum | solution.py:106
  267.1 2.6 copy.30
  269.7 2.5 copy.29
  272.2 5.4 %fusion.1 = f32[1024,512]{1,0:T(8,128)S(1)} fusion(f32[512,512]{1,0:T(8,128)} %get-tuple-element.14, f32[512,512]{1,0:T(8,128)} %copy-done.3, f32[512,512]{1,0:T(8,128)} %copy-done.2), kind=kOutput, calls=%fused_computation.10 | convolution fusion | flops 3221749760 | bytes 5242880 | tf_op jit(solution)/shard_map/dot_general | solution.py:93
  277.7 0.0 copy-done.6
  277.7 0.0 copy-done.7
  277.7 0.0 copy-start.5
  277.7 0.0 copy-start.14
  277.7 0.0 copy-start.16
  277.7 0.0 copy-start.17
  277.7 0.0 copy-start.20
  277.8 0.6 subtract_convert_fusion.1
  278.4 0.6 copy-done.5
  278.9 0.3 copy-done.14
  279.2 0.1 copy-done.16
  279.4 0.2 copy-done.17
  279.6 0.8 fusion.3
  280.3 0.4 copy-done.1
  280.8 0.1 copy-done.9
  280.9 0.3 copy-done.10
  281.2 0.1 copy-done.12
  281.4 0.2 copy-done.13
  281.5 1.8 fusion.42
  283.3 0.2 pad_maximum_fusion.2
  283.5 20.5 %convolution_convert_fusion = bf16[512,8192]{1,0:T(8,128)(2,1)} fusion(bf16[512,1536]{0,1:T(8,128)(2,1)S(1)} %bitcast.59, bf16[8192,1536]{0,1:T(8,128)(2,1)} %all-gather.10.cloned.1.call-done), kind=kOutput, calls=%fused_computation.6 | convolution fusion | flops 12889096192 | bytes 35127296 | tf_op jit(solution)/shard_map/dot_general | solution.py:115
  304.0 0.0 reduce-scatter.2.cloned.1.call-update
  304.0 1.0 copy-done.11
  305.1 1.0 copy.31
  306.1 77.8 %reduce-scatter.2.cloned.1.call-done = bf16[512,2048]{1,0:T(8,128)(2,1)} async-done(((bf16[512,8192]{1,0:T(8,128)(2,1)}), bf16[512,2048]{1,0:T(8,128)(2,1)}) %reduce-scatter.2.cloned.1.call-update) | async-done | bytes 2097168 | tf_op jit(solution)/shard_map/reduce_scatter | solution.py:116
  (33 shorter events, 0.2 us)
Async XLA Ops:
  7.2 19.1 %all-gather.6.cloned.1.call-start = ((), (), s32[]{:S(2)}) async-start(), calls=%async_computation.1 | async-start | bytes 2359296 | tf_op jit(solution)/shard_map/all_gather | solution.py:47
  9.5 119.0 %all-gather.8.cloned.1.call-start = ((), (), s32[]{:S(2)}) async-start(), calls=%async_computation.2 | async-start | bytes 13369344 | tf_op jit(solution)/shard_map/all_gather | solution.py:49
  28.3 145.6 %all-gather.10.cloned.1.call-start = ((), (), s32[]{:S(2)}) async-start(), calls=%async_computation.3 | async-start | bytes 37748736 | tf_op jit(solution)/shard_map/all_gather | solution.py:50
  128.6 1.0 copy-start.15
  128.6 2.1 copy-start.18
  128.6 125.7 %all-gather.12.cloned.1.call-start = ((), (), s32[]{:S(2)}) async-start(), calls=%async_computation.5 | async-start | bytes 2162688 | tf_op jit(solution)/shard_map/all_gather | solution.py:71
  193.3 1.0 copy-start.8
  209.1 174.7 %reduce-scatter.2.cloned.1.call-start = ((), (), s32[]{:S(2)}) async-start(), calls=%async_computation.4 | async-start | bytes 10485760 | tf_op jit(solution)/shard_map/reduce_scatter | solution.py:116
  213.3 13.9 %copy-start.2 = (f32[512,512]{1,0:T(8,128)}, f32[512,512]{1,0:T(8,128)S(1)}, u32[]{:S(2)}) copy-start(f32[512,512]{1,0:T(8,128)S(1)} %fusion.48) | copy-start | bytes 3145732
  213.3 13.9 %copy-start = (f32[512,512]{0,1:T(8,128)S(1)}, f32[512,512]{0,1:T(8,128)}, u32[]{:S(2)}) copy-start(f32[512,512]{0,1:T(8,128)} %get-tuple-element.27) | copy-start | bytes 3145732
  227.1 2.1 copy-start.3
  227.2 2.1 copy-start.4
  231.4 25.0 %copy-start.19 = (f32[16,512]{1,0:T(8,128)S(1)}, f32[16,512]{1,0:T(8,128)}, u32[]{:S(2)}) copy-start(f32[16,512]{1,0:T(8,128)} %param.8) | copy-start | bytes 98308
  272.2 5.5 %copy-start.6 = (f32[1024,512]{1,0:T(8,128)S(1)}, f32[1024,512]{1,0:T(8,128)}, u32[]{:S(2)}) copy-start(f32[1024,512]{1,0:T(8,128)} %fusion.12) | copy-start | bytes 6291460
  272.2 5.5 %copy-start.7 = (f32[1024,512]{1,0:T(8,128)S(1)}, f32[1024,512]{1,0:T(8,128)}, u32[]{:S(2)}) copy-start(f32[1024,512]{1,0:T(8,128)} %fusion.27) | copy-start | bytes 6291460
  277.7 1.2 copy-start.5
  277.7 1.5 copy-start.14
  277.7 1.7 copy-start.16
  277.7 1.8 copy-start.17
  277.7 1.8 copy-start.20
  279.5 1.2 copy-start.1
  279.5 1.4 copy-start.9
  279.5 1.7 copy-start.10
  279.5 1.8 copy-start.12
  279.6 2.0 copy-start.13
  304.0 1.0 copy-start.11
Sparse Core Ops, SparseCore 0:
  10.2 15.9 all-gather.5
  28.9 99.5 all-gather.7
  130.2 43.7 all-gather.9
  209.2 45.0 all-gather.11
  304.2 79.6 reduce-scatter.1
where the time goes:
time: 391 us; the launch traced here: 390 us
  waiting for transfers between devices  261 us (67%)
  matrix products  52.1 us (13%)
  other arithmetic  41.3 us (11%)
  local copies, waits for them, and re-layouts  21.6 us (6%)
  between operations  14.1 us (4%)
    all_gather x1, waiting for transfers between devices, local(): plane_w = lax.all_gather(mine_w, 'xy', axis=0, tiled=True)  100 us
    reduce_scatter x1, waiting for transfers between devices, local(): lax.psum_scatter(dx_terms.astype(bf16), 'chan', scatter_dimension=1, tile...  77.8 us
    all_gather x1, waiting for transfers between devices, local(): whole_w = lax.all_gather(plane_w, 'core', axis=1, tiled=True)  43.3 us
    all_gather x1, waiting for transfers between devices, local(): every = lax.all_gather(states, SEQ)  22.9 us
    dot_general x1, matrix products, local(): lax.dot_general(grad_proj, whole_w, contract, preferred_element_type=f32)  20.5 us
    dot_general x1, matrix products, local(): projected = jnp.dot(tokens, whole_w, preferred_element_type=f32)  19.4 us
    all_gather x1, waiting for transfers between devices, local(): pair_w = lax.all_gather(flat_w, 'core', axis=0, tiled=True)  16.7 us
    another operation x3, other arithmetic  14.4 us
  transfers between devices with their start and end apart: 5, of which 5 were waited for; matrix products, arithmetic and copies ran while one was open for 6% of the time, Pallas kernels for 0%

commit v1 on v0

--- a/solution.py
+++ b/solution.py
@@ -6,6 +6,11 @@
 
 f32 = jnp.float32
 bf16 = jnp.bfloat16
+
+
+def gather_over(x, name, dim):
+    sent = jnp.stack([x] * lax.axis_size(name))
+    return jnp.concatenate(lax.all_to_all(sent, name, 0, 0), axis=dim)
 
 
 def dft_tables(block_len, flip=False):
@@ -44,7 +49,7 @@
     me = lax.axis_index(SEQ)
     flat_w = proj_weight.reshape(proj_weight.shape[0], 3 * chan_count)
     half = 3 * chan_count // 2
-    pair_w = lax.all_gather(flat_w, "core", axis=0, tiled=True)
+    pair_w = gather_over(flat_w, "core", 0)
     mine_w = lax.dynamic_slice_in_dim(pair_w, lax.axis_index("core") * half, half, axis=1)
     plane_w = lax.all_gather(mine_w, "xy", axis=0, tiled=True)
     whole_w = lax.all_gather(plane_w, "core", axis=1, tiled=True)

time: 391 us -> 374 us (0.957)
  waiting for transfers between devices: 261 us -> 240 us
  starting transfers between devices: 0.38 us -> 5.39 us
    all_gather x1 -> x0, waiting for transfers between devices: 16.7 us -> none  [local(): pair_w = lax.all_gather(flat_w, 'core', axis=0, tiled=True)]
    all_gather x1, waiting for transfers between devices: 100 us -> 92.1 us  [local(): plane_w = lax.all_gather(mine_w, 'xy', axis=0, tiled=True)]
    all_to_all x0 -> x1, starting transfers between devices: none -> 5.08 us  [gather_over(): return jnp.concatenate(lax.all_to_all(sent, name, 0, 0), axis=dim)]
    another operation x3 -> x4, other arithmetic: 14.4 us -> 15.7 us
where the time goes in v1:
time: 374 us; the launch traced here: 373 us
  waiting for transfers between devices  240 us (64%)
  matrix products  50.7 us (14%)
  other arithmetic  42.6 us (11%)
  local copies, waits for them, and re-layouts  20.3 us (5%)
  between operations  14.1 us (4%)
  starting transfers between devices  5.39 us (1%)
    all_gather x1, waiting for transfers between devices, local(): plane_w = lax.all_gather(mine_w, 'xy', axis=0, tiled=True)  92.1 us
    reduce_scatter x1, waiting for transfers between devices, local(): lax.psum_scatter(dx_terms.astype(bf16), 'chan', scatter_dimension=1, tile...  77.8 us
    all_gather x1, waiting for transfers between devices, local(): whole_w = lax.all_gather(plane_w, 'core', axis=1, tiled=True)  45 us
    all_gather x1, waiting for transfers between devices, local(): every = lax.all_gather(states, SEQ)  22.9 us
    dot_general x1, matrix products, local(): projected = jnp.dot(tokens, whole_w, preferred_element_type=f32)  19.5 us
    dot_general x1, matrix products, local(): lax.dot_general(grad_proj, whole_w, contract, preferred_element_type=f32)  19.1 us
    another operation x3, other arithmetic  14.5 us
    reduce_sum x1, other arithmetic, local(): jnp.sum(into_b[:, None, :] * jnp.exp(-rates[:, None, :] * (tok_rows - ste...  10.7 us
  transfers between devices with their start and end apart: 5, of which 5 were waited for; matrix products, arithmetic and copies ran while one was open for 6% of the time, Pallas kernels for 0%

profile of v1, /device:TPU:1, one launch (start us, length us, event | category | flops | bytes accessed | tf_op | source)
XLA Modules:
  0.0 373.1 jit_solution(530419900369070687)
XLA Ops:
  7.2 1.4 copy.32
  8.6 1.3 pad_maximum_fusion.2
  9.9 5.1 %all-to-all-start = ((bf16[2,256,1536]{1,2,0:T(8,128)(2,1)}), bf16[2,256,1536]{1,2,0:T(8,128)(2,1)S(1)}, u32[]{:S(2)}, u32[]{:S(2)}) async-start(bf16[2,256,1536]{1,2,0:T(8,128)(2,1)} %pad_maximum_fusion.2), calls=%async_computation | async-start | bytes 3145728 | tf_op jit(solution)/shard_map/all_to_all | solution.py:13
  14.9 0.0 all-gather.5.cloned.1.call-start
  14.9 2.1 all-to-all-done
  17.1 0.7 copy.33
  17.8 0.9 constant_dynamic-slice_fusion
  18.7 0.0 all-gather.5.cloned.1.call-update
  18.7 0.0 all-gather.7.cloned.1.call-start
  18.8 92.1 %all-gather.5.cloned.1.call-done = bf16[8192,768]{1,0:T(8,128)(2,1)} async-done(((bf16[512,768]{1,0:T(8,128)(2,1)}), bf16[8192,768]{1,0:T(8,128)(2,1)}) %all-gather.5.cloned.1.call-update) | async-done | bytes 12582928 | tf_op jit(solution)/shard_map/all_gather | solution.py:54
  110.9 0.0 all-gather.7.cloned.1.call-update
  110.9 0.0 all-gather.9.cloned.1.call-start
  111.0 1.0 copy-done.15
  112.0 1.0 copy.35
  113.0 0.0 copy-done.18
  113.0 45.0 %all-gather.7.cloned.1.call-done = bf16[8192,1536]{1,0:T(8,128)(2,1)} async-done(((bf16[8192,768]{1,0:T(8,128)(2,1)}), bf16[8192,1536]{1,0:T(8,128)(2,1)}) %all-gather.7.cloned.1.call-update) | async-done | bytes 25165840 | tf_op jit(solution)/shard_map/all_gather | solution.py:55
  158.0 19.5 %fusion = bf16[512,1536]{0,1:T(8,128)(2,1)S(1)} fusion(bf16[8192,1536]{1,0:T(8,128)(2,1)} %all-gather.7.cloned.1.call-done, bf16[512,8192]{1,0:T(8,128)(2,1)} %param.6), kind=kOutput, calls=%fused_computation.8 | convolution fusion | flops 12885688320 | bytes 35127296 | tf_op jit(solution)/shard_map/dot_general | solution.py:56
  177.5 0.0 copy-start.8
  177.5 0.4 convert.56
  177.9 0.6 copy-done.8
  178.5 1.8 convert_multiply_fusion.1
  180.3 2.6 copy.36
  182.9 2.5 copy.34
  185.4 7.2 %multiply_reduce_fusion.3 = (f32[16,512]{1,0:T(8,128)S(1)}, f32[16,512]{1,0:T(8,128)S(1)}) fusion(f32[512,512]{1,0:T(8,128)} %copy.34, f32[512]{0:T(512)S(1)} %iota_subtract_fusion.2, f32[16,512]{1,0:T(8,128)S(1)} %get-tuple-element.34, f32[512,512]{1,0:T(8,128)} %copy.36), kind=kLoop, calls=%fused_computation.3 | loop fusion | flops 25149440 | bytes 2197504 | tf_op jit(solution)/shard_map/reduce_sum | solution.py:73
  192.6 0.6 pad_maximum_fusion.4
  193.2 0.0 all-gather.9.cloned.1.call-update
  193.3 0.2 reduce-scatter.2.cloned.1.call-start
  193.6 3.8 %fusion.48 = f32[512,512]{1,0:T(8,128)S(1)} fusion(), kind=kLoop, calls=%fused_computation.87 | loop fusion | flops 3670016 | bytes 1048576 | tf_op jit(solution)/shard_map/cos | solution.py:24
  197.4 0.0 copy-start.2
  197.4 0.0 copy-start
  197.4 4.1 %fusion.41 = bf16[512,512]{1,0:T(8,128)(2,1)S(1)} fusion(f32[512]{0:T(512)S(1)} %fusion.57, s32[512]{0:T(512)S(1)} %iota_subtract_fusion.1, pred[512]{0:T(512)(128)(4,1)S(1)} %iota_compare_fusion), kind=kLoop, calls=%fused_computation.80 | loop fusion | flops 3932160 | bytes 528896 | tf_op jit(solution)/shard_map/convert.10
  201.5 9.8 %multiply_convert_fusion.3 = (bf16[512,512]{1,0:T(8,128)(2,1)}, bf16[512,512]{1,0:T(8,128)(2,1)}, bf16[512,512]{1,0:T(8,128)(2,1)}, f32[512,512]{1,0:T(8,128)S(1...) fusion(f32[512]{0:T(512)S(1)} %get-tuple-element.43, s32[512]{0:T(512)S(1)} %iota_subtract_fusion.1, ...), kind=kLoop, calls=%fused_computation.66 | loop fusion | flops 10223616 | bytes 3678720 | tf_op jit(solution)/shard_map/convert.11
  211.3 0.0 copy-done.2
  211.3 0.0 copy-done
  211.3 0.0 copy-start.4
  211.3 2.1 fusion.12
  213.4 0.0 copy-done.3
  213.4 2.1 fusion.27
  215.5 22.9 %all-gather.9.cloned.1.call-done = f32[64,16,512]{2,1,0:T(8,128)} async-done(((f32[2,16,512]{2,1,0:T(8,128)}), f32[64,16,512]{2,1,0:T(8,128)}) %all-gather.9.cloned.1.call-update) | async-done | bytes 2097168 | tf_op jit(solution)/shard_map/all_gather | solution.py:76
  238.5 2.1 fusion.15
  240.5 0.0 copy-done.19
  240.6 10.7 %multiply_reduce_fusion = (f32[512,512]{1,0:T(8,128)}, f32[512,512]{1,0:T(8,128)}, f32[512,512]{1,0:T(8,128)}) fusion(f32[512]{0:T(512)S(1)} %get-tuple-element.41, f32[16,512]{1,0:T(8,128)S(1)} %mul.373, f32[16,512]{1,0:T(8,128)S(1)} %get-tuple-element.34, f32[512]{0:T(512)S(1)} %get-tuple-element.42, f32[16,512]{1,0:T(8,128)S(1)} %get-tuple-element.19, ...), kind=kLoop, calls=%fused_computation | loop fusion | flops 36962304 | bytes 3280896 | tf_op jit(solution)/shard_map/reduce_sum | solution.py:111
  251.3 2.6 copy.39
  253.8 2.5 copy.38
  256.4 5.4 %fusion.1 = f32[1024,512]{1,0:T(8,128)S(1)} fusion(f32[512,512]{1,0:T(8,128)} %get-tuple-element.16, f32[512,512]{1,0:T(8,128)} %copy-done.3, f32[512,512]{1,0:T(8,128)} %copy-done.2), kind=kOutput, calls=%fused_computation.10 | convolution fusion | flops 3221749760 | bytes 5242880 | tf_op jit(solution)/shard_map/dot_general | solution.py:98
  261.9 0.0 copy-start.20
  261.9 0.6 subtract_convert_fusion.1
  262.5 0.6 copy-done.5
  263.1 0.3 copy-done.14
  263.4 0.1 copy-done.16
  263.5 0.2 copy-done.17
  263.7 0.8 fusion.3
  264.5 0.4 copy-done.1
  264.9 0.1 copy-done.9
  265.0 0.3 copy-done.10
  265.4 0.1 copy-done.12
  265.5 0.2 copy-done.13
  265.7 1.8 fusion.42
  267.4 0.2 pad_maximum_fusion.3
  267.6 19.1 %convolution_convert_fusion = bf16[512,8192]{1,0:T(8,128)(2,1)} fusion(bf16[512,1536]{0,1:T(8,128)(2,1)S(1)} %bitcast.61, bf16[8192,1536]{1,0:T(8,128)(2,1)} %all-gather.7.cloned.1.call-done), kind=kOutput, calls=%fused_computation.6 | convolution fusion | flops 12889096192 | bytes 35127296 | tf_op jit(solution)/shard_map/dot_general | solution.py:120
  286.7 0.0 reduce-scatter.2.cloned.1.call-update
  286.8 1.0 copy-done.11
  287.8 1.0 copy.40
  288.8 77.8 %reduce-scatter.2.cloned.1.call-done = bf16[512,2048]{1,0:T(8,128)(2,1)} async-done(((bf16[512,8192]{1,0:T(8,128)(2,1)}), bf16[512,2048]{1,0:T(8,128)(2,1)}) %reduce-scatter.2.cloned.1.call-update) | async-done | bytes 2097168 | tf_op jit(solution)/shard_map/reduce_scatter | solution.py:121
  (34 shorter events, 0.2 us)
Async XLA Ops:
  9.9 7.2 %all-to-all-start = ((bf16[2,256,1536]{1,2,0:T(8,128)(2,1)}), bf16[2,256,1536]{1,2,0:T(8,128)(2,1)S(1)}, u32[]{:S(2)}, u32[]{:S(2)}) async-start(bf16[2,256,1536]{1,2,0:T(8,128)(2,1)} %pad_maximum_fusion.2), calls=%async_computation | async-start | bytes 3145728 | tf_op jit(solution)/shard_map/all_to_all | solution.py:13
  14.9 96.0 %all-gather.5.cloned.1.call-start = ((), (), s32[]{:S(2)}) async-start(), calls=%async_computation.2 | async-start | bytes 13369344 | tf_op jit(solution)/shard_map/all_gather | solution.py:54
  18.7 139.3 %all-gather.7.cloned.1.call-start = ((), (), s32[]{:S(2)}) async-start(), calls=%async_computation.3 | async-start | bytes 37748736 | tf_op jit(solution)/shard_map/all_gather | solution.py:55
  110.9 1.0 copy-start.15
  110.9 2.1 copy-start.18
  110.9 127.5 %all-gather.9.cloned.1.call-start = ((), (), s32[]{:S(2)}) async-start(), calls=%async_computation.5 | async-start | bytes 2162688 | tf_op jit(solution)/shard_map/all_gather | solution.py:76
  177.5 1.0 copy-start.8
  193.3 173.3 %reduce-scatter.2.cloned.1.call-start = ((), (), s32[]{:S(2)}) async-start(), calls=%async_computation.4 | async-start | bytes 10485760 | tf_op jit(solution)/shard_map/reduce_scatter | solution.py:121
  197.4 13.9 %copy-start.2 = (f32[512,512]{1,0:T(8,128)}, f32[512,512]{1,0:T(8,128)S(1)}, u32[]{:S(2)}) copy-start(f32[512,512]{1,0:T(8,128)S(1)} %fusion.48) | copy-start | bytes 3145732
  197.4 13.9 %copy-start = (f32[512,512]{0,1:T(8,128)S(1)}, f32[512,512]{0,1:T(8,128)}, u32[]{:S(2)}) copy-start(f32[512,512]{0,1:T(8,128)} %get-tuple-element.29) | copy-start | bytes 3145732
  211.3 2.1 copy-start.3
  211.3 2.1 copy-start.4
  215.5 25.0 %copy-start.19 = (f32[16,512]{1,0:T(8,128)S(1)}, f32[16,512]{1,0:T(8,128)}, u32[]{:S(2)}) copy-start(f32[16,512]{1,0:T(8,128)} %param.8) | copy-start | bytes 98308
  256.4 5.5 %copy-start.6 = (f32[1024,512]{1,0:T(8,128)S(1)}, f32[1024,512]{1,0:T(8,128)}, u32[]{:S(2)}) copy-start(f32[1024,512]{1,0:T(8,128)} %fusion.12) | copy-start | bytes 6291460
  256.4 5.5 %copy-start.7 = (f32[1024,512]{1,0:T(8,128)S(1)}, f32[1024,512]{1,0:T(8,128)}, u32[]{:S(2)}) copy-start(f32[1024,512]{1,0:T(8,128)} %fusion.27) | copy-start | bytes 6291460
  261.8 1.2 copy-start.5
  261.9 1.5 copy-start.14
  261.9 1.7 copy-start.16
  261.9 1.8 copy-start.17
  261.9 1.8 copy-start.20
  263.7 1.2 copy-start.1
  263.7 1.4 copy-start.9
  263.7 1.7 copy-start.10
  263.7 1.8 copy-start.12
  263.7 2.0 copy-start.13
  286.7 1.0 copy-start.11
Sparse Core Ops, SparseCore 0:
  18.8 92.0 all-gather.4
  112.6 45.3 all-gather.6
  193.4 45.0 all-gather.8
  286.9 79.6 reduce-scatter.1
